TPU v7x, 128 devices: a whole 4x4x4 slice. The times are simulated.
128 devices in a mesh: req: 8 (over x, core), exp: 16 (over y, z).
Axes of the slice: x: 4, y: 4, z: 4, core: 2. Of those that a mesh axis runs over, the one named last changes fastest.
Arguments:
- queries: bfloat16 [8192, 2048], P('req', 'exp'), may hold values from -6 to 6
- keys: bfloat16 [8192, 2048], P('req', 'exp'), may hold values from -15 to 15
- values: bfloat16 [8192, 2048], P('req', 'exp'), may hold values from -6 to 6
- prefix_keys: bfloat16 [4, 4096, 2048], P(None, 'req', 'exp'), may hold values from -15 to 15
- prefix_values: bfloat16 [4, 4096, 2048], P(None, 'req', 'exp'), may hold values from -6 to 6
- lengths: int32 [8, 8], P('req'), may hold values from 1 to 512, 1024 in all within a row
- groups: int32 [8, 8], P('req'), may hold values from 0 to 3
- residual: bfloat16 [8192, 2048], P(('req', 'exp')), may hold values from -6 to 6
- out_proj: bfloat16 [2048, 2048], P('exp'), may hold values from -0.125 to 0.125
- norm_gain: bfloat16 [2048], replicated, may hold values from 0.099609375 to 1.8984375
- expert_ids: int32 [8192, 4], P(('req', 'exp')), may hold values from 0 to 31, all different within a row; in each aligned block of 64 rows (0 to 63, 64 to 127, ...) at most 16 rows name the same one
- expert_gates: bfloat16 [8192, 4], P(('req', 'exp')), may hold values from 0.049804688 to 0.5
- w_gate: bfloat16 [32, 2048, 704], P('exp'), may hold values from -0.125 to 0.125
- w_up: bfloat16 [32, 2048, 704], P('exp'), may hold values from -0.125 to 0.125
- w_down: bfloat16 [32, 704, 2048], P('exp'), may hold values from -0.21875 to 0.21875
Outputs:
- layer_out: bfloat16 [8192, 2048], P(('req', 'exp'))
Inputs may be any that keep to these rules, and one draw needn't show every extreme that they name: The 8 lengths of a row sum to 1024; the longest request of each row has half of 1024 tokens. `expert_ids`: each row names 4 different experts. Among the 64 tokens of one device, no expert is named more than 16 times; on some device some expert is named exactly 16 times.
All inputs are finite; a program needn't handle non-finite values.
Results may differ from a plain program's by a relative error of at most 0.02.
Values may be sent and summed in bfloat16 or wider, within the bound.
A program may use at most 256 MiB of HBM per device.

v0:
```python
import math
import jax
import jax.numpy as jnp
from jax import lax
from jax.sharding import PartitionSpec as P

HEAD = 128
TOPK = 4
EXPERTS = 32
G = 4
RQ = 8
ROW_TOK = 1024
NEG = -1e30


def token_layout(lengths, groups):
    req_ends = jnp.cumsum(lengths, axis=-1)
    starts = req_ends - lengths
    position = jnp.arange(ROW_TOK, dtype=jnp.int32)
    request = jnp.sum((position[None, :, None] >= req_ends[:, None, :]).astype(jnp.int32), axis=-1)
    onehot = request[:, :, None] == jnp.arange(RQ, dtype=jnp.int32)[None, None, :]
    first_tok = jnp.sum(jnp.where(onehot, starts[:, None, :], 0), axis=-1)
    tok_group = jnp.sum(jnp.where(onehot, groups[:, None, :], 0), axis=-1)
    return (request, position[None, :] - first_tok, tok_group)


def split_blocks(row_count):
    if row_count % 1024 == 0 and row_count > 1024:
        return row_count // 1024
    return 1


def pack_parts(parts):
    return jnp.concatenate([parts[0], parts[1], parts[2]], axis=1)


def unpack_parts(packed, head_count):
    columns = head_count * HEAD
    return (
        packed[:, :columns],
        packed[:, columns : columns + head_count],
        packed[:, columns + head_count :],
    )


def attend_prefix(query_rows, query_group, prefix_k, prefix_v):
    row_count, columns = query_rows.shape
    head_count = columns // HEAD
    span = prefix_k.shape[1]
    key_grid = prefix_k.reshape(G, span, head_count, HEAD)
    val_grid = prefix_v.reshape(G, span, head_count, HEAD)
    blocks = split_blocks(row_count)
    block_len = row_count // blocks
    scaling = 1.0 / math.sqrt(HEAD)

    def per_block(pieces):
        block_q, block_g = pieces
        query_grid = block_q.reshape(block_len, head_count, HEAD)
        scores = (
            jnp.einsum("qhd,gkhd->hqgk", query_grid, key_grid, preferred_element_type=jnp.float32)
            * scaling
        )
        member = block_g[:, None] == jnp.arange(G, dtype=jnp.int32)[None, :]
        scores = jnp.where(member[None, :, :, None], scores, NEG)
        maxima = jnp.max(scores, axis=(2, 3))
        exp_terms = jnp.exp(scores - maxima[:, :, None, None])
        totals = jnp.sum(exp_terms, axis=(2, 3))
        weighted = jnp.einsum(
            "hqgk,gkhd->qhd",
            exp_terms.astype(jnp.bfloat16),
            val_grid,
            preferred_element_type=jnp.float32,
        )
        return (weighted.reshape(block_len, columns), maxima.T, totals.T)

    weighted, maxima, totals = lax.map(
        per_block,
        (query_rows.reshape(blocks, block_len, columns), query_group.reshape(blocks, block_len)),
    )
    return (
        weighted.reshape(row_count, columns),
        maxima.reshape(row_count, head_count),
        totals.reshape(row_count, head_count),
    )


def attend_suffix(queries, keys, values, request, position):
    row_count, columns = queries.shape
    head_count = columns // HEAD
    blocks = split_blocks(row_count)
    block_len = row_count // blocks
    scaling = 1.0 / math.sqrt(HEAD)
    key_grid = keys.reshape(row_count, head_count, HEAD)
    val_grid = values.reshape(row_count, head_count, HEAD)

    def per_block(pieces):
        block_q, block_req, block_pos = pieces
        query_grid = block_q.reshape(block_len, head_count, HEAD)
        scores = (
            jnp.einsum("qhd,khd->hqk", query_grid, key_grid, preferred_element_type=jnp.float32)
            * scaling
        )
        allowed = (request[None, :] == block_req[:, None]) & (
            position[None, :] <= block_pos[:, None]
        )
        scores = jnp.where(allowed[None, :, :], scores, NEG)
        maxima = jnp.max(scores, axis=2)
        exp_terms = jnp.exp(scores - maxima[:, :, None])
        totals = jnp.sum(exp_terms, axis=2)
        weighted = jnp.einsum(
            "hqk,khd->qhd",
            exp_terms.astype(jnp.bfloat16),
            val_grid,
            preferred_element_type=jnp.float32,
        )
        return (weighted.reshape(block_len, columns), maxima.T, totals.T)

    weighted, maxima, totals = lax.map(
        per_block,
        (
            queries.reshape(blocks, block_len, columns),
            request.reshape(blocks, block_len),
            position.reshape(blocks, block_len),
        ),
    )
    return (
        weighted.reshape(row_count, columns),
        maxima.reshape(row_count, head_count),
        totals.reshape(row_count, head_count),
    )


def combine(former, latter):
    weighted_a, maxima_a, totals_a = former
    weighted_b, maxima_b, totals_b = latter
    row_count, head_count = maxima_a.shape
    maxima = jnp.maximum(maxima_a, maxima_b)
    factor_a = jnp.exp(maxima_a - maxima)
    factor_b = jnp.exp(maxima_b - maxima)
    weighted = (
        weighted_a.reshape(row_count, head_count, HEAD) * factor_a[:, :, None]
        + weighted_b.reshape(row_count, head_count, HEAD) * factor_b[:, :, None]
    )
    return (
        weighted.reshape(row_count, head_count * HEAD),
        maxima,
        totals_a * factor_a + totals_b * factor_b,
    )


def per_device(
    queries,
    keys,
    values,
    prefix_keys,
    prefix_values,
    lengths,
    groups,
    residual,
    out_proj,
    norm_gain,
    expert_ids,
    expert_gates,
    w_gate,
    w_up,
    w_down,
):
    row_tok, columns = queries.shape
    head_count = columns // HEAD
    tok_dev = residual.shape[0]
    request, position, tok_group = token_layout(lengths, groups)
    request, position, tok_group = (request[0], position[0], tok_group[0])
    all_groups = lax.all_gather(tok_group, "req", axis=0, tiled=True)
    partial_value = pack_parts(
        attend_prefix(
            lax.all_gather(queries, "req", axis=0, tiled=True),
            all_groups,
            prefix_keys,
            prefix_values,
        )
    )
    returned = lax.all_to_all(partial_value, "req", split_axis=0, concat_axis=0, tiled=True)
    owners = returned.shape[0] // row_tok
    back_w, back_m, back_t = unpack_parts(returned, head_count)
    all_weighted = back_w.reshape(owners, row_tok, head_count, HEAD)
    all_maxima = back_m.reshape(owners, row_tok, head_count)
    all_totals = back_t.reshape(owners, row_tok, head_count)
    maxima = jnp.max(all_maxima, axis=0)
    factor = jnp.exp(all_maxima - maxima[None])
    weighted = jnp.sum(all_weighted * factor[..., None], axis=0).reshape(row_tok, columns)
    prefix_part = (weighted, maxima, jnp.sum(all_totals * factor, axis=0))
    suffix_part = attend_suffix(queries, keys, values, request, position)
    weighted, maxima, totals = combine(prefix_part, suffix_part)
    attended = (
        (weighted.reshape(row_tok, head_count, HEAD) / totals[:, :, None])
        .reshape(row_tok, columns)
        .astype(jnp.bfloat16)
    )
    projected = lax.psum_scatter(
        jnp.dot(attended, out_proj, preferred_element_type=jnp.float32),
        "exp",
        scatter_dimension=0,
        tiled=True,
    )
    stream = residual.astype(jnp.float32) + projected
    meansq = jnp.mean(stream * stream, axis=-1, keepdims=True)
    normed = (stream * lax.rsqrt(meansq + 1e-06) * norm_gain.astype(jnp.float32)).astype(
        jnp.bfloat16
    )
    capacity = max(2, tok_dev // 4)
    flat_ids = expert_ids.reshape(-1)
    onehot = (flat_ids[:, None] == jnp.arange(EXPERTS, dtype=jnp.int32)[None, :]).astype(jnp.int32)
    slot_of = jnp.sum(onehot * (jnp.cumsum(onehot, axis=0) - 1), axis=1)
    source_rows = jnp.arange(tok_dev * TOPK, dtype=jnp.int32) // TOPK
    buffer = (
        jnp.zeros((EXPERTS, capacity, normed.shape[1]), jnp.bfloat16)
        .at[flat_ids, slot_of]
        .set(normed[source_rows])
    )
    exp_count = lax.axis_size("exp")
    exp_dev = w_gate.shape[0]
    received = lax.all_to_all(buffer, "exp", split_axis=0, concat_axis=0, tiled=True)
    slots = received.shape[1]
    grid_in = received.reshape(exp_count, exp_dev, slots, received.shape[2])
    gate_h = jnp.einsum("secd,edf->secf", grid_in, w_gate, preferred_element_type=jnp.float32)
    up_h = jnp.einsum("secd,edf->secf", grid_in, w_up, preferred_element_type=jnp.float32)
    hidden = (jax.nn.silu(gate_h) * up_h).astype(jnp.bfloat16)
    expert_out = jnp.einsum("secf,efd->secd", hidden, w_down, preferred_element_type=jnp.float32)
    returned = lax.all_to_all(
        expert_out.reshape(EXPERTS, slots, received.shape[2]),
        "exp",
        split_axis=0,
        concat_axis=0,
        tiled=True,
    )
    gathered = returned[flat_ids, slot_of] * expert_gates.reshape(-1).astype(jnp.float32)[:, None]
    mixture = jnp.sum(gathered.reshape(tok_dev, TOPK, gathered.shape[1]), axis=1)
    return (stream + mixture).astype(jnp.bfloat16)


def solution(mesh):
    in_specs = (
        P("req", "exp"),
        P("req", "exp"),
        P("req", "exp"),
        P(None, "req", "exp"),
        P(None, "req", "exp"),
        P("req", None),
        P("req", None),
        P(("req", "exp"), None),
        P("exp", None),
        P(),
        P(("req", "exp"), None),
        P(("req", "exp"), None),
        P("exp", None, None),
        P("exp", None, None),
        P("exp", None, None),
    )
    out_specs = P(("req", "exp"), None)
    return jax.shard_map(
        per_device, mesh=mesh, in_specs=in_specs, out_specs=out_specs, check_vma=False
    )
```

profile of v0, /device:TPU:0, one launch (start us, length us, event | category | flops | bytes accessed | tf_op | source)
XLA Modules:
  0.0 431.7 jit_solution(6236507258747720294)
XLA Ops:
  9.6 13.3 %all_gather.6 = s32[8192]{0:T(1024)S(1)} all-gather(s32[1024]{0:T(1024)S(1)} %get-tuple-element.81), channel_id=1, replica_groups=mesh['req'=8,'exp'=16] {'req'}, dimensions={0}, use_global_device_ids=true | all-gather | bytes 36864 | tf_op jit(solution)/shard_map/all_gather | solution.py:173
  22.9 13.8 %all-gather.2.cloned.1.call-done = bf16[8192,128]{1,0:T(8,128)(2,1)} async-done(((bf16[1024,128]{1,0:T(8,128)(2,1)}), bf16[8192,128]{1,0:T(8,128)(2,1)}) %all-gather.2.cloned.1.call-update) | async-done | bytes 2097168 | tf_op jit(solution)/shard_map/all_gather | solution.py:176
  36.7 55.2 %while.2 = (s32[]{:T(128)}, f32[8,1024,128]{1,2,0:T(8,128)}, f32[8,1024,1]{1,2,0:T(1,128)S(1)}, f32[8,1024,1]{1,2,0:T(1,128)S(1)}, s32[8,1024]{1,0:T(8,128)S(1)}...) while((s32[]{:T(128)}, f32[8,1024,128]{1,2,0:T(8,128)}, ...), condition=%wide.region_6.7_spmd, body=%wide.region_3.6_spmd.sunk | while | flops 1096812544 | bytes 29160576 | solution.py:76
  40.9 2.7 fusion.100
  43.6 2.4 fusion.99
  47.7 2.7 fusion.100
  54.7 2.8 fusion.100
  57.4 2.4 fusion.99
  61.6 2.7 fusion.100
  68.5 2.7 fusion.100
  75.4 2.7 fusion.100
  78.1 2.4 fusion.99
  82.3 2.7 fusion.100
  85.0 2.4 fusion.99
  89.2 2.8 fusion.100
  91.9 4.9 %pad_maximum_fusion = f32[8,1024,130]{1,2,0:T(8,128)} fusion(f32[8,1024,1]{1,2,0:T(1,128)S(1)} %get-tuple-element.78, f32[8,1024,1]{1,2,0:T(1,128)S(1)} %get-tuple-element.77, f32[8,1024,128]{1,2,0:T(8,128)} %get-tuple-element.76), kind=kLoop, calls=%fused_computation.30 | loop fusion | flops 2129920 | bytes 8519680 | tf_op jit(solution)/shard_map/concatenate | solution.py:34
  96.9 4.7 %all-to-all-start = ((f32[8,1024,130]{1,2,0:T(8,128)}), f32[8,1024,130]{1,2,0:T(8,128)}, u32[]{:S(2)}, u32[]{:S(2)}) async-start(f32[8,1024,130]{1,2,0:T(8,128)} %pad_maximum_fusion), calls=%async_computation | async-start | bytes 8912896 | tf_op jit(solution)/shard_map/all_to_all | solution.py:182
  105.8 48.2 %all-to-all-done = f32[8,1024,130]{1,2,0:T(8,128)} async-done(((f32[8,1024,130]{1,2,0:T(8,128)}), f32[8,1024,130]{1,2,0:T(8,128)}, u32[]{:S(2)}, u32[]{:S(2)}) %all-to-all-start) | async-done | bytes 4259872 | tf_op jit(solution)/shard_map/all_to_all | solution.py:182
  154.1 4.7 %copy.101 = f32[8,1024,130]{1,0,2:T(8,128)S(1)} copy(f32[8,1024,130]{1,2,0:T(8,128)} %all-to-all-done) | data formatting | bytes 8519680 | tf_op jit(solution)/shard_map/all_to_all | solution.py:182
  159.1 3.9 copy.89
  165.6 5.6 %copy.90 = f32[16,8,8,1024]{3,2,1,0:T(8,128)S(1)} copy(f32[16,8,8,1024]{3,1,2,0:T(8,128)} %bitcast.182) | data formatting | bytes 8388608
  173.0 8.2 %fusion.71 = f32[1024,2048]{1,0:T(8,128)} fusion(bf16[128,2048]{1,0:T(8,128)(2,1)S(1)} %copy-done, bf16[1024,128]{1,0:T(8,128)(2,1)S(1)} %copy-done.5, f32[1024,1024]{0,1:T(8,128)} %copy-done.1, f32[1024]{0:T(1024)S(1)} %get-tuple-element.109, f32[1024,128]{1,0:T(8,128)S(1)} %copy.68, f32[1024]{0:T(1024)S(1)} %get-tuple-element.99, ...), kind=kOutput, calls=%fused_computation.58 | convolution fusion | flops 808058880 | bytes 13910016 | tf_op jit(solution)/shard_map/dot_general | solution.py:200
  183.3 82.6 %reduce-scatter.2.cloned.1.call-done = f32[64,2048]{1,0:T(8,128)} async-done(((f32[1024,2048]{1,0:T(8,128)}), f32[64,2048]{1,0:T(8,128)}) %reduce-scatter.2.cloned.1.call-update) | async-done | bytes 524304 | tf_op jit(solution)/shard_map/reduce_scatter | solution.py:199
  270.9 33.3 %scatter_fusion = bf16[32,16,2048]{2,1,0:T(8,128)(2,1)S(1)} fusion(bf16[32,16,2048]{2,1,0:T(8,128)(2,1)S(1)} %broadcast_in_dim.105, s32[256]{0:T(256)S(1)} %bitcast.180, bf16[256,2048]{1,0:T(8,128)(2,1)} %gather_fusion), kind=kCustom, calls=%fused_computation.2 | custom fusion | bytes 3147776 | tf_op jit(solution)/shard_map/scatter | solution.py:218
  304.2 32.2 %all_to_all.19 = bf16[32,16,2048]{2,1,0:T(8,128)(2,1)S(1)} all-to-all(bf16[32,16,2048]{2,1,0:T(8,128)(2,1)S(1)} %scatter_fusion), channel_id=1, replica_groups=mesh['req'=8,'exp'=16] {'exp'}, dimensions={0} | all-to-all | bytes 4194304 | tf_op jit(solution)/shard_map/all_to_all | solution.py:222
  337.7 4.5 %fusion.24 = f32[2,16,16,704]{3,2,1,0:T(8,128)S(1)} fusion(bf16[2,2048,704]{1,2,0:T(8,128)(2,1)} %param.29, bf16[16,2,16,2048]{3,2,1,0:T(8,128)(2,1)S(1)} %bitcast.184), kind=kOutput, calls=%fused_computation.28 | convolution fusion | flops 1476395008 | bytes 9306112 | tf_op jit(solution)/shard_map/secd,edf->secf/dot_general | solution.py:225
  342.1 10.6 %fusion.29 = f32[16,2,16,2048]{3,2,0,1:T(8,128)} fusion(bf16[2,704,2048]{2,1,0:T(8,128)(2,1)} %param.31, f32[2,16,16,704]{3,2,1,0:T(8,128)S(1)} %fusion.24, bf16[2,2048,704]{1,2,0:T(8,128)(2,1)} %param.30, bf16[16,2,16,2048]{3,2,1,0:T(8,128)(2,1)} %bitcast.185), kind=kOutput, calls=%fused_computation.38 | convolution fusion | flops 2954952704 | bytes 19267584 | tf_op jit(solution)/shard_map/secf,efd->secd/dot_general | solution.py:228
  352.7 4.7 %copy.75 = f32[16,2,16,2048]{3,2,1,0:T(8,128)} copy(f32[16,2,16,2048]{3,2,0,1:T(8,128)} %fusion.29) | data formatting | bytes 8388608 | tf_op jit(solution)/shard_map/secf,efd->secd/transpose | solution.py:228
  357.4 4.7 %all-to-all-start.2 = ((f32[32,16,2048]{2,1,0:T(8,128)}), f32[32,16,2048]{2,1,0:T(8,128)}, u32[]{:S(2)}, u32[]{:S(2)}) async-start(f32[32,16,2048]{2,1,0:T(8,128)} %bitcast.183), calls=%async_computation.3 | async-start | bytes 8388608 | tf_op jit(solution)/shard_map/all_to_all | solution.py:229
  362.2 52.8 %all-to-all-done.2 = f32[32,16,2048]{2,1,0:T(8,128)} async-done(((f32[32,16,2048]{2,1,0:T(8,128)}), f32[32,16,2048]{2,1,0:T(8,128)}, u32[]{:S(2)}, u32[]{:S(2)}) %all-to-all-start.2) | async-done | bytes 4194336 | tf_op jit(solution)/shard_map/all_to_all | solution.py:229
  415.0 4.0 gather_fusion.1
  420.7 3.2 multiply_reduce_fusion
  (123 shorter events, 46.3 us)
Async XLA Ops:
  6.5 166.4 %copy-start = (bf16[128,2048]{1,0:T(8,128)(2,1)S(1)}, bf16[128,2048]{1,0:T(8,128)(2,1)}, u32[]{:S(2)}) copy-start(bf16[128,2048]{1,0:T(8,128)(2,1)} %param.25) | copy-start | bytes 1572868
  6.5 30.2 %all-gather.2.cloned.1.call-start = ((), (), s32[]{:S(2)}) async-start(), calls=%async_computation.4 | async-start | bytes 2359296 | tf_op jit(solution)/shard_map/all_gather | solution.py:176
  39.1 1.7 copy-start.10
  46.0 1.7 copy-start.10
  52.9 1.7 copy-start.10
  59.8 1.7 copy-start.10
  66.7 1.7 copy-start.10
  73.6 1.7 copy-start.10
  80.5 1.7 copy-start.10
  87.4 1.7 copy-start.10
  96.9 5.2 %copy-start.6 = (bf16[1024,128]{1,0:T(8,128)(2,1)S(1)}, bf16[1024,128]{1,0:T(8,128)(2,1)}, u32[]{:S(2)}) copy-start(bf16[1024,128]{1,0:T(8,128)(2,1)} %param.17) | copy-start | bytes 786436
  96.9 5.3 %copy-start.11 = (bf16[1024,128]{1,0:T(8,128)(2,1)S(1)}, bf16[1024,128]{1,0:T(8,128)(2,1)}, u32[]{:S(2)}) copy-start(bf16[1024,128]{1,0:T(8,128)(2,1)} %param.18) | copy-start | bytes 786436
  96.9 57.2 %all-to-all-start = ((f32[8,1024,130]{1,2,0:T(8,128)}), f32[8,1024,130]{1,2,0:T(8,128)}, u32[]{:S(2)}, u32[]{:S(2)}) async-start(f32[8,1024,130]{1,2,0:T(8,128)} %pad_maximum_fusion), calls=%async_computation | async-start | bytes 8912896 | tf_op jit(solution)/shard_map/all_to_all | solution.py:182
  101.6 164.3 %reduce-scatter.2.cloned.1.call-start = ((), (), s32[]{:S(2)}) async-start(), calls=%async_computation.5 | async-start | bytes 8912896 | tf_op jit(solution)/shard_map/reduce_scatter | solution.py:199
  103.2 2.0 copy-start.1
  171.2 1.7 copy-start.5
  181.2 0.7 copy-start.8
  181.2 1.1 copy-start.7
  181.2 84.7 %copy-start.3 = (bf16[64,2048]{1,0:T(8,128)(2,1)S(1)}, bf16[64,2048]{1,0:T(8,128)(2,1)}, u32[]{:S(2)}) copy-start(bf16[64,2048]{1,0:T(8,128)(2,1)} %param.24) | copy-start | bytes 786436
  336.3 1.3 copy-start.4
  357.4 4.7 %copy-start.9 = (bf16[64,4]{0,1:T(4,128)(2,1)S(1)}, bf16[64,4]{0,1:T(4,128)(2,1)}, u32[]{:S(2)}) copy-start(bf16[64,4]{0,1:T(4,128)(2,1)} %param.28) | copy-start | bytes 1540
  357.4 57.6 %all-to-all-start.2 = ((f32[32,16,2048]{2,1,0:T(8,128)}), f32[32,16,2048]{2,1,0:T(8,128)}, u32[]{:S(2)}, u32[]{:S(2)}) async-start(f32[32,16,2048]{2,1,0:T(8,128)} %bitcast.183), calls=%async_computation.3 | async-start | bytes 8388608 | tf_op jit(solution)/shard_map/all_to_all | solution.py:229
  419.0 4.9 %copy-start.2 = (f32[64,2048]{1,0:T(8,128)S(1)}, f32[64,2048]{1,0:T(8,128)}, u32[]{:S(2)}) copy-start(f32[64,2048]{1,0:T(8,128)} %reduce-scatter.2.cloned.1.call-done) | copy-start | bytes 1572868
Sparse Core Ops, SparseCore 0:
  9.1 27.5 all-gather.1
  181.3 84.5 reduce-scatter.1
where the time goes:
time: 438 us; the launch traced here: 432 us
  waiting for transfers between devices  198 us (45%)
  local copies, waits for them, and re-layouts  68.4 us (16%)
  matrix products  65.4 us (15%)
  blocking collectives  45.4 us (10%)
  other arithmetic  30.3 us (7%)
  between operations  14 us (3%)
  starting transfers between devices  9.88 us (2%)
    reduce_scatter x1, waiting for transfers between devices, per_device(): lax.psum_scatter(jnp.dot(attended, out_proj, preferred_element_type=jnp.f...  82.6 us
    all_to_all x1, waiting for transfers between devices, per_device(): lax.all_to_all(expert_out.reshape(EXPERTS, slots, received.shape[2]), 'ex...  52.8 us
    all_to_all x1, waiting for transfers between devices, per_device(): lax.all_to_all(partial_value, 'req', split_axis=0, concat_axis=0, tiled=T...  48.2 us
    scatter x1, local copies, waits for them, and re-layouts, per_device(): buffer = jnp.zeros((EXPERTS, capacity, normed.shape[1]), jnp.bfloat16).at...  33.3 us
    all_to_all x1, blocking collectives, per_device(): lax.all_to_all(buffer, 'exp', split_axis=0, concat_axis=0, tiled=True)  32.2 us
    dot_general x8, matrix products, per_block(): jnp.einsum('hqgk,gkhd->qhd', exp_terms.astype(jnp.bfloat16), val_grid, pr...  21.9 us
    dot_general x8, matrix products, per_block(): jnp.einsum('qhd,gkhd->hqgk', query_grid, key_grid, preferred_element_type...  19.1 us
    unnamed x26, local copies, waits for them, and re-layouts  13.9 us
  transfers between devices with their start and end apart: 4, of which 4 were waited for; matrix products, arithmetic and copies ran while one was open for 1% of the time, Pallas kernels for 0%

commit v1 on v0

--- a/solution.py
+++ b/solution.py
@@ -170,7 +170,14 @@
     tok_dev = residual.shape[0]
     request, position, tok_group = token_layout(lengths, groups)
     request, position, tok_group = (request[0], position[0], tok_group[0])
-    all_groups = lax.all_gather(tok_group, "req", axis=0, tiled=True)
+    n_dev = lax.axis_size("req")
+    right = [(i, (i + 1) % n_dev) for i in range(n_dev)]
+    shards = [tok_group]
+    for stride in range(1, n_dev):
+        shards = [lax.ppermute(shards[0], "req", right), *shards]
+    whole = jnp.concatenate(shards, axis=0)
+    shift = (lax.axis_index("req") + 1) * shards[-1].shape[0]
+    all_groups = jnp.roll(whole, shift, axis=0)
     partial_value = pack_parts(
         attend_prefix(
             lax.all_gather(queries, "req", axis=0, tiled=True),

time: 438 us -> 442 us (level)
  waiting for transfers between devices: 198 us -> 216 us
  blocking collectives: 45.4 us -> 31.9 us
    ppermute x0 -> x7, waiting for transfers between devices: none -> 29.7 us  [per_device(): shards = [lax.ppermute(shards[0], 'req', right), *shards]]
    all_gather x1, waiting for transfers between devices: 13.8 us -> 0.02 us  [per_device(): lax.all_gather(queries, 'req', axis=0, tiled=True)]
    all_gather x1 -> x0, blocking collectives: 13.3 us -> none  [per_device(): all_groups = lax.all_gather(tok_group, 'req', axis=0, tiled=True)]
    unnamed x26 -> x41, local copies, waits for them, and re-layouts: 13.9 us -> 13.9 us
  transfers between devices with their start and end apart: 4 -> 11, of which waited for: 4 -> 10; matrix products, arithmetic and copies ran while one was open for 1% -> 1% of each run, Pallas kernels for 0% -> 0%
where the time goes in v1:
time: 442 us; the launch traced here: 436 us
  waiting for transfers between devices  216 us (49%)
  local copies, waits for them, and re-layouts  68.5 us (15%)
  matrix products  65.4 us (15%)
  blocking collectives  31.9 us (7%)
  other arithmetic  30.3 us (7%)
  between operations  14.1 us (3%)
  starting transfers between devices  9.91 us (2%)
    reduce_scatter x1, waiting for transfers between devices, per_device(): lax.psum_scatter(jnp.dot(attended, out_proj, preferred_element_type=jnp.f...  84.1 us
    all_to_all x1, waiting for transfers between devices, per_device(): lax.all_to_all(expert_out.reshape(EXPERTS, slots, received.shape[2]), 'ex...  52.9 us
    all_to_all x1, waiting for transfers between devices, per_device(): lax.all_to_all(partial_value, 'req', split_axis=0, concat_axis=0, tiled=T...  48.2 us
    scatter x1, local copies, waits for them, and re-layouts, per_device(): buffer = jnp.zeros((EXPERTS, capacity, normed.shape[1]), jnp.bfloat16).at...  33.3 us
    all_to_all x1, blocking collectives, per_device(): lax.all_to_all(buffer, 'exp', split_axis=0, concat_axis=0, tiled=True)  31.9 us
    ppermute x7, waiting for transfers between devices, per_device(): shards = [lax.ppermute(shards[0], 'req', right), *shards]  29.7 us
    dot_general x8, matrix products, per_block(): jnp.einsum('hqgk,gkhd->qhd', exp_terms.astype(jnp.bfloat16), val_grid, pr...  21.9 us
    dot_general x8, matrix products, per_block(): jnp.einsum('qhd,gkhd->hqgk', query_grid, key_grid, preferred_element_type...  19.1 us
  transfers between devices with their start and end apart: 11, of which 10 were waited for; matrix products, arithmetic and copies ran while one was open for 1% of the time, Pallas kernels for 0%

profile of v1, /device:TPU:0, one launch (start us, length us, event | category | flops | bytes accessed | tf_op | source)
XLA Modules:
  0.0 435.9 jit_solution(1285087541836410994)
XLA Ops:
  9.6 4.2 collective-permute-done
  13.8 4.2 collective-permute-done.1
  18.1 4.2 collective-permute-done.2
  22.3 4.2 collective-permute-done.3
  26.6 4.2 collective-permute-done.4
  30.8 4.2 collective-permute-done.5
  35.1 4.2 collective-permute-done.6
  39.5 55.3 %while.2 = (s32[]{:T(128)}, f32[8,1024,128]{1,2,0:T(8,128)}, f32[8,1024,1]{1,2,0:T(1,128)S(1)}, f32[8,1024,1]{1,2,0:T(1,128)S(1)}, s32[8,1024]{1,0:T(8,128)S(1)}...) while((s32[]{:T(128)}, f32[8,1024,128]{1,2,0:T(8,128)}, ...), condition=%wide.region_6.7_spmd, body=%wide.region_3.6_spmd.sunk | while | flops 1096812544 | bytes 29160576 | solution.py:76
  50.6 2.7 fusion.100
  57.5 2.8 fusion.100
  64.4 2.7 fusion.100
  71.3 2.7 fusion.100
  78.2 2.7 fusion.100
  85.1 2.7 fusion.100
  92.0 2.8 fusion.100
  94.8 4.9 %pad_maximum_fusion = f32[8,1024,130]{1,2,0:T(8,128)} fusion(f32[8,1024,1]{1,2,0:T(1,128)S(1)} %get-tuple-element.78, f32[8,1024,1]{1,2,0:T(1,128)S(1)} %get-tuple-element.77, f32[8,1024,128]{1,2,0:T(8,128)} %get-tuple-element.76), kind=kLoop, calls=%fused_computation.30 | loop fusion | flops 2129920 | bytes 8519680 | tf_op jit(solution)/shard_map/concatenate | solution.py:34
  99.7 4.7 %all-to-all-start = ((f32[8,1024,130]{1,2,0:T(8,128)}), f32[8,1024,130]{1,2,0:T(8,128)}, u32[]{:S(2)}, u32[]{:S(2)}) async-start(f32[8,1024,130]{1,2,0:T(8,128)} %pad_maximum_fusion), calls=%async_computation | async-start | bytes 8912896 | tf_op jit(solution)/shard_map/all_to_all | solution.py:189
  108.7 48.2 %all-to-all-done = f32[8,1024,130]{1,2,0:T(8,128)} async-done(((f32[8,1024,130]{1,2,0:T(8,128)}), f32[8,1024,130]{1,2,0:T(8,128)}, u32[]{:S(2)}, u32[]{:S(2)}) %all-to-all-start) | async-done | bytes 4259872 | tf_op jit(solution)/shard_map/all_to_all | solution.py:189
  156.9 4.7 %copy.101 = f32[8,1024,130]{1,0,2:T(8,128)S(1)} copy(f32[8,1024,130]{1,2,0:T(8,128)} %all-to-all-done) | data formatting | bytes 8519680 | tf_op jit(solution)/shard_map/all_to_all | solution.py:189
  162.0 3.9 copy.89
  168.5 5.6 %copy.90 = f32[16,8,8,1024]{3,2,1,0:T(8,128)S(1)} copy(f32[16,8,8,1024]{3,1,2,0:T(8,128)} %bitcast.182) | data formatting | bytes 8388608
  175.8 8.2 %fusion.71 = f32[1024,2048]{1,0:T(8,128)} fusion(bf16[128,2048]{1,0:T(8,128)(2,1)S(1)} %copy-done, bf16[1024,128]{1,0:T(8,128)(2,1)S(1)} %copy-done.5, f32[1024,1024]{0,1:T(8,128)} %copy-done.1, f32[1024]{0:T(1024)S(1)} %get-tuple-element.109, f32[1024,128]{1,0:T(8,128)S(1)} %copy.68, f32[1024]{0:T(1024)S(1)} %get-tuple-element.99, ...), kind=kOutput, calls=%fused_computation.58 | convolution fusion | flops 808058880 | bytes 13910016 | tf_op jit(solution)/shard_map/dot_general | solution.py:207
  186.1 84.1 %reduce-scatter.2.cloned.1.call-done = f32[64,2048]{1,0:T(8,128)} async-done(((f32[1024,2048]{1,0:T(8,128)}), f32[64,2048]{1,0:T(8,128)}) %reduce-scatter.2.cloned.1.call-update) | async-done | bytes 524304 | tf_op jit(solution)/shard_map/reduce_scatter | solution.py:206
  275.2 33.3 %scatter_fusion = bf16[32,16,2048]{2,1,0:T(8,128)(2,1)S(1)} fusion(bf16[32,16,2048]{2,1,0:T(8,128)(2,1)S(1)} %broadcast_in_dim.105, s32[256]{0:T(256)S(1)} %bitcast.180, bf16[256,2048]{1,0:T(8,128)(2,1)} %gather_fusion), kind=kCustom, calls=%fused_computation.2 | custom fusion | bytes 3147776 | tf_op jit(solution)/shard_map/scatter | solution.py:225
  308.5 31.9 %all_to_all.19 = bf16[32,16,2048]{2,1,0:T(8,128)(2,1)S(1)} all-to-all(bf16[32,16,2048]{2,1,0:T(8,128)(2,1)S(1)} %scatter_fusion), channel_id=1, replica_groups=mesh['req'=8,'exp'=16] {'exp'}, dimensions={0} | all-to-all | bytes 4194304 | tf_op jit(solution)/shard_map/all_to_all | solution.py:229
  341.8 4.5 %fusion.24 = f32[2,16,16,704]{3,2,1,0:T(8,128)S(1)} fusion(bf16[2,2048,704]{1,2,0:T(8,128)(2,1)} %param.29, bf16[16,2,16,2048]{3,2,1,0:T(8,128)(2,1)S(1)} %bitcast.184), kind=kOutput, calls=%fused_computation.28 | convolution fusion | flops 1476395008 | bytes 9306112 | tf_op jit(solution)/shard_map/secd,edf->secf/dot_general | solution.py:232
  346.2 10.6 %fusion.29 = f32[16,2,16,2048]{3,2,0,1:T(8,128)} fusion(bf16[2,704,2048]{2,1,0:T(8,128)(2,1)} %param.31, f32[2,16,16,704]{3,2,1,0:T(8,128)S(1)} %fusion.24, bf16[2,2048,704]{1,2,0:T(8,128)(2,1)} %param.30, bf16[16,2,16,2048]{3,2,1,0:T(8,128)(2,1)} %bitcast.185), kind=kOutput, calls=%fused_computation.38 | convolution fusion | flops 2954952704 | bytes 19267584 | tf_op jit(solution)/shard_map/secf,efd->secd/dot_general | solution.py:235
  356.8 4.7 %copy.75 = f32[16,2,16,2048]{3,2,1,0:T(8,128)} copy(f32[16,2,16,2048]{3,2,0,1:T(8,128)} %fusion.29) | data formatting | bytes 8388608 | tf_op jit(solution)/shard_map/secf,efd->secd/transpose | solution.py:235
  361.5 4.7 %all-to-all-start.2 = ((f32[32,16,2048]{2,1,0:T(8,128)}), f32[32,16,2048]{2,1,0:T(8,128)}, u32[]{:S(2)}, u32[]{:S(2)}) async-start(f32[32,16,2048]{2,1,0:T(8,128)} %bitcast.183), calls=%async_computation.3 | async-start | bytes 8388608 | tf_op jit(solution)/shard_map/all_to_all | solution.py:236
  366.3 52.9 %all-to-all-done.2 = f32[32,16,2048]{2,1,0:T(8,128)} async-done(((f32[32,16,2048]{2,1,0:T(8,128)}), f32[32,16,2048]{2,1,0:T(8,128)}, u32[]{:S(2)}, u32[]{:S(2)}) %all-to-all-start.2) | async-done | bytes 4194336 | tf_op jit(solution)/shard_map/all_to_all | solution.py:236
  419.1 4.0 gather_fusion.1
  424.9 3.2 multiply_reduce_fusion
  (153 shorter events, 58.7 us)
Async XLA Ops:
  6.5 169.3 %copy-start = (bf16[128,2048]{1,0:T(8,128)(2,1)S(1)}, bf16[128,2048]{1,0:T(8,128)(2,1)}, u32[]{:S(2)}) copy-start(bf16[128,2048]{1,0:T(8,128)(2,1)} %param.25) | copy-start | bytes 1572868
  6.5 33.0 %all-gather.2.cloned.1.call-start = ((), (), s32[]{:S(2)}) async-start(), calls=%async_computation.4 | async-start | bytes 2359296 | tf_op jit(solution)/shard_map/all_gather | solution.py:183
  9.6 4.3 collective-permute-start
  13.8 4.2 collective-permute-start.1
  18.1 4.2 collective-permute-start.2
  22.3 4.2 collective-permute-start.3
  26.6 4.2 collective-permute-start.4
  30.8 4.2 collective-permute-start.5
  35.1 4.2 collective-permute-start.6
  42.0 1.7 copy-start.10
  48.9 1.7 copy-start.10
  55.8 1.7 copy-start.10
  62.7 1.7 copy-start.10
  69.6 1.7 copy-start.10
  76.5 1.7 copy-start.10
  83.4 1.7 copy-start.10
  90.3 1.7 copy-start.10
  99.7 5.2 %copy-start.6 = (bf16[1024,128]{1,0:T(8,128)(2,1)S(1)}, bf16[1024,128]{1,0:T(8,128)(2,1)}, u32[]{:S(2)}) copy-start(bf16[1024,128]{1,0:T(8,128)(2,1)} %param.17) | copy-start | bytes 786436
  99.7 5.3 %copy-start.11 = (bf16[1024,128]{1,0:T(8,128)(2,1)S(1)}, bf16[1024,128]{1,0:T(8,128)(2,1)}, u32[]{:S(2)}) copy-start(bf16[1024,128]{1,0:T(8,128)(2,1)} %param.18) | copy-start | bytes 786436
  99.7 57.2 %all-to-all-start = ((f32[8,1024,130]{1,2,0:T(8,128)}), f32[8,1024,130]{1,2,0:T(8,128)}, u32[]{:S(2)}, u32[]{:S(2)}) async-start(f32[8,1024,130]{1,2,0:T(8,128)} %pad_maximum_fusion), calls=%async_computation | async-start | bytes 8912896 | tf_op jit(solution)/shard_map/all_to_all | solution.py:189
  104.5 165.8 %reduce-scatter.2.cloned.1.call-start = ((), (), s32[]{:S(2)}) async-start(), calls=%async_computation.5 | async-start | bytes 8912896 | tf_op jit(solution)/shard_map/reduce_scatter | solution.py:206
  106.1 2.0 copy-start.1
  174.1 1.7 copy-start.5
  184.0 0.7 copy-start.8
  184.0 1.1 copy-start.7
  184.0 86.2 %copy-start.3 = (bf16[64,2048]{1,0:T(8,128)(2,1)S(1)}, bf16[64,2048]{1,0:T(8,128)(2,1)}, u32[]{:S(2)}) copy-start(bf16[64,2048]{1,0:T(8,128)(2,1)} %param.24) | copy-start | bytes 786436
  340.4 1.3 copy-start.4
  361.5 4.7 %copy-start.9 = (bf16[64,4]{0,1:T(4,128)(2,1)S(1)}, bf16[64,4]{0,1:T(4,128)(2,1)}, u32[]{:S(2)}) copy-start(bf16[64,4]{0,1:T(4,128)(2,1)} %param.28) | copy-start | bytes 1540
  361.5 57.7 %all-to-all-start.2 = ((f32[32,16,2048]{2,1,0:T(8,128)}), f32[32,16,2048]{2,1,0:T(8,128)}, u32[]{:S(2)}, u32[]{:S(2)}) async-start(f32[32,16,2048]{2,1,0:T(8,128)} %bitcast.183), calls=%async_computation.3 | async-start | bytes 8388608 | tf_op jit(solution)/shard_map/all_to_all | solution.py:236
  423.2 4.9 %copy-start.2 = (f32[64,2048]{1,0:T(8,128)S(1)}, f32[64,2048]{1,0:T(8,128)}, u32[]{:S(2)}) copy-start(f32[64,2048]{1,0:T(8,128)} %reduce-scatter.2.cloned.1.call-done) | copy-start | bytes 1572868
Sparse Core Ops, SparseCore 0:
  9.1 27.6 all-gather.1
  184.2 86.0 reduce-scatter.1
